TPU v7x, 32 devices: a whole 2x2x4 slice. The times are simulated.
32 devices in a mesh: groups: 2 (over y), tiles: 8 (over z, core), ens: 2 (over x), lev: 1.
Axes of the slice: x: 2, y: 2, z: 4, core: 2. Of those that a mesh axis runs over, the one named last changes fastest.
Arguments:
- inputs: bfloat16 [2, 1, 16, 3, 32, 32, 128], P('ens', 'lev', ('groups', 'tiles')), parts along dimension 2, may hold values from -6 to 6
- slot_rows: int32 [16, 3], P('groups'), parts along dimension 0, may hold values from -1 to 3, as said below
- cell_mask: int32 [1, 16, 3, 32, 32], P('lev', ('groups', 'tiles')), parts along dimension 1, may hold values 0 or 1
- target: bfloat16 [1, 16, 3, 4, 32, 32], P('lev', ('groups', 'tiles')), parts along dimension 1, may hold values from -24 to 24
- dw_kernel: float32 [7, 7, 128], replicated, may hold values from -0.875 to 0.875
- dw_bias: float32 [128], replicated, may hold values from -3 to 3
- ln_gain: float32 [128], replicated, may hold values from 0.1 to 1.9
- ln_bias: float32 [128], replicated, may hold values from -3 to 3
- w_in: bfloat16 [128, 256], replicated, may hold values from -0.5 to 0.5
- b_in: float32 [256], replicated, may hold values from -3 to 3
- w_out: bfloat16 [256, 128], replicated, may hold values from -0.375 to 0.375
- b_out: float32 [128], replicated, may hold values from -3 to 3
- layer_scale: float32 [128], replicated, may hold values from 0.3 to 1.5
- w_head: float32 [128, 4], replicated, may hold values from -2 to 2
Outputs:
- grad_x: bfloat16 [2, 1, 16, 3, 32, 32, 128], P('ens', 'lev', ('groups', 'tiles')), parts along dimension 2
- crps: bfloat16 [1, 16, 3, 32, 32], P('lev', ('groups', 'tiles'), None, 'ens'), parts along dimension 1
There are 2 independent parts, one for each index of `groups`. A program takes and returns all parts, laid end to end along the dimension named above; an argument that names none is the same for every part. Nothing has to cross between parts.
Inputs may be any that keep to these rules, and one draw needn't show every extreme that they name: `slot_rows`: each row c lists the tile rows of the ocean tiles of tile column c in increasing order, each at most once, followed by -1 in the empty slots. Tile columns c and c + 4 hold 4 ocean tiles together; every column holds 1 to 3, and some column holds exactly 3.
All inputs are finite; a program needn't handle non-finite values. No bound on the sum of `cell_mask` on one device may be relied on, other than what follows from the above.
Results may differ from a plain program's by a relative error of at most 0.012.
Values may be sent and summed in bfloat16 or wider, within the bound.
A program may use at most 64 MiB of HBM per device.

v0:
```python
import jax
import jax.numpy as jnp
from jax import lax
from jax.sharding import PartitionSpec as P

softness = 0.0625
epsilon = 1e-06
highest = lax.Precision.HIGHEST


def padded_2(block, sides, width):
    for axis, dim in sides:
        count = lax.axis_size(axis)
        forward = [(i, i + 1) for i in range(count - 1)]
        forward.append((count - 1, 0))
        backward = [(target, source) for source, target in forward]
        low = lax.ppermute(
            lax.slice_in_dim(block, block.shape[dim] - width, None, axis=dim), axis, forward
        )
        high = lax.ppermute(lax.slice_in_dim(block, 0, width, axis=dim), axis, backward)
        block = jnp.concatenate([low, block, high], axis=dim)
    return block


def soft_abs(value):
    return jnp.sqrt(value * value + softness)


def soft_sign(value):
    return value / jnp.sqrt(value * value + softness)


def gelu_slope(value):
    cumulative = 0.5 * (1.0 + lax.erf(value * 0.7071067811865476))
    return cumulative + value * jnp.exp(-0.5 * value * value) * 0.3989422804014327


def match_rows(target_rows, source_rows, offset):
    hits = (
        (source_rows[None, :] == target_rows[:, None] + offset)
        & (source_rows[None, :] >= 0)
        & (target_rows[:, None] >= 0)
    )
    return hits.astype(jnp.bfloat16)


def pick_tiles(selector, data):
    return jnp.einsum("st,tabc->sabc", selector, data, preferred_element_type=jnp.float32).astype(
        jnp.bfloat16
    )


def column_block(center, own_rows, rim):
    tile = center.shape[1]
    above = pick_tiles(match_rows(own_rows, own_rows, -1), center[:, tile - rim :])
    below = pick_tiles(match_rows(own_rows, own_rows, 1), center[:, :rim])
    return jnp.concatenate([above, center, below], axis=1)


def one_side(strips, own_rows, side_rows, rim):
    tile = strips.shape[1]
    upper = pick_tiles(match_rows(own_rows, side_rows, -1), strips[:, tile - rim :])
    level = pick_tiles(match_rows(own_rows, side_rows, 0), strips)
    lower = pick_tiles(match_rows(own_rows, side_rows, 1), strips[:, :rim])
    return jnp.concatenate([upper, level, lower], axis=1)


def side_strips(extended, own_rows, west_rows, east_rows, rim):
    west_in = extended[:, :, :rim]
    east_in = extended[:, :, extended.shape[2] - rim :]
    return (
        one_side(west_in, own_rows, west_rows, rim),
        one_side(east_in, own_rows, east_rows, rim),
    )


def stencil(padded, weights, breadth):
    size = weights.shape[0]
    height = padded.shape[1] - size + 1
    total = jnp.zeros((padded.shape[0], height, breadth, padded.shape[3]), jnp.float32)
    for row_off in range(size):
        for col_off in range(size):
            window = padded[:, row_off : row_off + height, col_off : col_off + breadth]
            total = total + weights[row_off, col_off] * window.astype(jnp.float32)
    return total


def convolve(middle, left, right, weights):
    tile = middle.shape[2]
    result = stencil(jnp.concatenate([left, middle, right], axis=2), weights, tile)
    return result


def member_grad(mine, every, observed, weight_mask, members):
    spread = jnp.sum(soft_sign(mine[:, None] - every[None]), axis=1)
    return weight_mask[None, :, None] * (
        soft_sign(mine - observed[None]) / members - spread / (members * members)
    )


def crps_map(every, observed, weight_mask, members):
    skill = jnp.sum(soft_abs(every - observed[None]), axis=0) / members
    spread = jnp.sum(soft_abs(every[:, None] - every[None]), axis=(0, 1)) / (2 * members * members)
    return weight_mask * jnp.sum(skill - spread, axis=1)


def ensemble_terms(pred, observed, weight_mask):
    members = lax.axis_size("ens")
    member = lax.axis_index("ens")
    tile = pred.shape[2]
    share = tile // members
    every = lax.all_gather(pred[None], "ens", axis=0, tiled=True)
    grad_pred = member_grad(pred[None], every, observed, weight_mask, members)[0].astype(
        jnp.bfloat16
    )
    score = lax.dynamic_slice_in_dim(
        crps_map(every, observed, weight_mask, members), member * share, share, 1
    ).astype(jnp.bfloat16)
    return (grad_pred, score)


def head_back(grad_pred, w_head, width):
    count_tiles = grad_pred.shape[0]
    tile = grad_pred.shape[2]
    flat = grad_pred.astype(jnp.float32).transpose(0, 2, 3, 1).reshape(-1, grad_pred.shape[1])
    return jnp.dot(flat, w_head.T, precision=highest).reshape(count_tiles, tile, tile, width)


def on_device(
    inputs,
    slot_rows,
    cell_mask,
    target,
    dw_kernel,
    dw_bias,
    ln_gain,
    ln_bias,
    w_in,
    b_in,
    w_out,
    b_out,
    layer_scale,
    w_head,
):
    columns = lax.axis_size("tiles")
    column = lax.axis_index("tiles")
    center_x = inputs[0, 0, 0]
    tile = center_x.shape[1]
    width = center_x.shape[3]
    rim = dw_kernel.shape[0] // 2
    own_rows = lax.dynamic_index_in_dim(slot_rows, column, 0, keepdims=False)
    west_rows = lax.dynamic_index_in_dim(
        slot_rows, (column + columns - 1) % columns, 0, keepdims=False
    )
    east_rows = lax.dynamic_index_in_dim(slot_rows, (column + 1) % columns, 0, keepdims=False)
    live = own_rows >= 0
    live_mask = cell_mask[0, 0].astype(jnp.float32) * live[:, None, None].astype(jnp.float32)
    mask_half = live_mask.astype(jnp.bfloat16)
    masked_x = center_x * mask_half[:, :, :, None]
    observed_all = target[0, 0]
    edges = jnp.concatenate([masked_x[:, :, :rim], masked_x[:, :, tile - rim :]], axis=2)
    extended = padded_2(edges, (("tiles", 2),), rim)
    middle = column_block(masked_x, own_rows, rim)
    left, right = side_strips(extended, own_rows, west_rows, east_rows, rim)
    conv_out = convolve(middle, left, right, dw_kernel) + dw_bias
    mean_z = jnp.mean(conv_out, axis=-1, keepdims=True)
    centered = conv_out - mean_z
    inv_std = lax.rsqrt(jnp.mean(centered * centered, axis=-1, keepdims=True) + epsilon)
    normed = centered * inv_std
    features = (normed * ln_gain + ln_bias).astype(jnp.bfloat16)
    residual_head = jnp.dot(
        masked_x.reshape(-1, width).astype(jnp.float32), w_head, precision=highest
    )
    count_tiles = features.shape[0]
    pre = jnp.dot(features.reshape(-1, width), w_in, preferred_element_type=jnp.float32) + b_in
    act = jax.nn.gelu(pre, approximate=False).astype(jnp.bfloat16)
    branch = jnp.dot(act, w_out, preferred_element_type=jnp.float32) + b_out
    pred = residual_head + jnp.dot(layer_scale * branch, w_head, precision=highest)
    pred = pred.reshape(count_tiles, tile, tile, -1).transpose(0, 3, 1, 2)
    grad_pred, score = ensemble_terms(pred, observed_all.astype(jnp.float32), live_mask)
    grad_rows = head_back(grad_pred, w_head, width)
    scaled = (layer_scale * grad_rows.reshape(-1, width)).astype(jnp.bfloat16)
    grad_act = jnp.dot(scaled, w_out.T, preferred_element_type=jnp.float32)
    grad_pre = (grad_act * gelu_slope(pre)).astype(jnp.bfloat16)
    grad_feat = jnp.dot(grad_pre, w_in.T, preferred_element_type=jnp.float32).astype(jnp.bfloat16)
    grad_feat, grad_pred, score, grad_rows = (
        grad_feat.reshape(count_tiles, tile, tile, width),
        grad_pred,
        score,
        grad_rows,
    )
    gated = grad_feat.astype(jnp.float32) * ln_gain
    grad_z = (
        inv_std
        * (
            gated
            - jnp.mean(gated, axis=-1, keepdims=True)
            - normed * jnp.mean(gated * normed, axis=-1, keepdims=True)
        )
    ).astype(jnp.bfloat16)
    back_edges = jnp.concatenate([grad_z[:, :, :rim], grad_z[:, :, tile - rim :]], axis=2)
    back_extended = padded_2(back_edges, (("tiles", 2),), rim)
    back_middle = column_block(grad_z, own_rows, rim)
    back_left, back_right = side_strips(back_extended, own_rows, west_rows, east_rows, rim)
    through = convolve(back_middle, back_left, back_right, dw_kernel[::-1, ::-1])
    grad_x = (live_mask[:, :, :, None] * (grad_rows + through)).astype(jnp.bfloat16)
    return (grad_x[None, None, None], score[None, None])


def solution(mesh):
    placed = (
        P("ens", "lev", ("groups", "tiles"), None, None, None, None),
        P("groups", None),
        P("lev", ("groups", "tiles"), None, None, None),
        P("lev", ("groups", "tiles"), None, None, None, None),
        P(),
        P(),
        P(),
        P(),
        P(),
        P(),
        P(),
        P(),
        P(),
        P(),
    )
    return jax.shard_map(
        on_device,
        mesh=mesh,
        in_specs=placed,
        out_specs=(
            P("ens", "lev", ("groups", "tiles"), None, None, None, None),
            P("lev", ("groups", "tiles"), None, "ens", None),
        ),
        check_vma=False,
    )
```

profile of v0, /device:TPU:0, one launch (start us, length us, event | category | flops | bytes accessed | tf_op | source)
XLA Modules:
  0.0 85.4 jit_solution(16133979632700640904)
XLA Ops:
  0.7 1.0 %dynamic-slice_reduce_fusion.1 = (s32[3]{0:T(128)S(1)}, s32[3]{0:T(128)S(1)}, s32[3]{0:T(128)S(1)}) fusion(s32[8,3]{0,1:T(4,128)} %param.15, s32[]{:T(128)S(6)} %select_n.26, s32[]{:T(128)S(6)} %select_n.24, s32[]{:T(128)S(6)} %select_n.28), kind=kLoop, calls=%fused_computation.170 | loop fusion | bytes 84 | tf_op jit(solution)/shard_map/jit(dynamic_index_in_dim)/dynamic_slice | solution.py:152
  1.8 0.9 %fusion.117 = (bf16[3,32,32]{2,1,0:T(8,128)(2,1)S(1)}, f32[3,32,32]{2,1,0:T(8,128)S(1)}) fusion(f32[3]{0:T(128)S(1)} %get-tuple-element.107, s32[1,1,3,32,32]{4,3,2,1,0:T(8,128)} %param.16), kind=kLoop, calls=%fused_computation.261 | loop fusion | flops 9216 | bytes 30732 | tf_op jit(solution)/shard_map/convert_element_type | solution.py:158
  2.7 1.6 %bitcast_multiply_fusion = bf16[3,32,32,128]{3,2,1,0:T(8,128)(2,1)S(1)} fusion(bf16[1,1,1,3,32,32,128]{6,5,4,3,2,1,0:T(8,128)(2,1)} %param.14, bf16[3,32,32]{2,1,0:T(8,128)(2,1)S(1)} %get-tuple-element.20), kind=kLoop, calls=%fused_computation.73 | loop fusion | flops 393216 | bytes 1579008 | tf_op jit(solution)/shard_map/mul | solution.py:159
  4.4 0.5 collective-permute-start
  4.9 4.1 %collective-permute-start.1 = (bf16[3,32,3,128]{3,2,1,0:T(4,128)(2,1)S(1)}, bf16[3,32,3,128]{3,2,1,0:T(4,128)(2,1)S(1)}, u32[]{:S(2)}, u32[]{:S(2)}) collective-permute-start(bf16[3,32,3,128]{3,2,1,0:T(4,128)(2,1)S(1)} %get-tuple-element.31), channel_id=1, source_target_pairs={{2,0},{4,2},{6,4},{8,6},{10,8},{12,10},{14,12},{0,14},{3,1},{5,3},... | collective-permute-start | bytes 221192 | tf_op jit(solution)/shard_map/ppermute | solution.py:20
  9.0 0.2 compare_reduce_fusion.2
  9.7 0.5 bitcast_multiply_fusion.1
  10.2 0.1 and_and_fusion.2
  10.3 0.2 fusion.41
  10.5 0.2 fusion.39
  10.8 0.7 fusion.126
  11.7 0.1 fusion.62
  11.8 0.2 fusion.43
  12.0 0.1 fusion.60
  12.2 0.2 fusion.37
  12.5 0.1 fusion.58
  12.6 0.1 fusion.56
  12.8 1.9 %maximum_maximum_fusion = (bf16[3,38,35,128]{3,2,1,0:T(8,128)(2,1)S(1)}, bf16[3,38,35,128]{3,2,1,0:T(8,128)(2,1)S(1)}) fusion(bf16[3,3,32,128]{3,2,1,0:T(8,128)(2,1)S(1)} %copy.150, bf16[3,32,32,128]{3,2,1,0:T(8,128)(2,1)S(1)} %bitcast_multiply_fusion, bf16[3,3,32,128]{3,2,1,0:T(8,128)(2,1)S(1)} %copy.151, bf16[3,3,3,128]{3,2,1,0:T(4,128)(2,1)S(1)} %copy.158, ...), kind=kLoop, calls=%fused_computation.41 | loop fusion | flops 12257280 | bytes 3151872 | tf_op jit(solution)/shard_map/concatenate | solution.py:90
  14.9 13.6 %fusion.116 = (f32[3,32,32]{2,1,0:T(8,128)S(1)}, f32[3,32,32,128]{3,2,1,0:T(8,128)S(1)}) fusion(f32[128]{0:T(128)S(1)} %copy-done.64, bf16[3,38,35,128]{3,2,1,0:T(8,128)(2,1)S(1)} %get-tuple-element.25, f32[128]{0:T(128)S(1)} %get-tuple-element.89, f32[128]{0:T(128)S(1)} %get-tuple-element.90, f32[128]{0:T(128)S(1)} %get-tuple-element.43, ...), kind=kLoop, calls=%fused_computation.260 | loop fusion | flops 60552192 | bytes 35574784 | tf_op jit(solution)/shard_map/reduce_sum | solution.py:166
  28.5 0.9 %multiply_reduce_fusion.2 = f32[3,32,32]{2,1,0:T(8,128)S(1)} fusion(f32[3,32,32,128]{3,2,1,0:T(8,128)S(1)} %get-tuple-element.19, f32[3,32,32]{2,1,0:T(8,128)S(1)} %broadcast_multiply_fusion.1), kind=kLoop, calls=%fused_computation.38 | loop fusion | flops 1176576 | bytes 1597440 | tf_op jit(solution)/shard_map/reduce_sum | solution.py:168
  29.5 1.2 %add_convert_fusion = bf16[3,32,32,128]{3,2,1,0:T(8,128)(2,1)S(1)} fusion(f32[3,32,32,128]{3,2,1,0:T(8,128)S(1)} %get-tuple-element.19, f32[128]{0:T(128)S(1)} %copy-done.47, f32[128]{0:T(128)S(1)} %copy-done.11, f32[3,32,32]{2,1,0:T(8,128)S(1)} %add_rsqrt_fusion, f32[3,32,32]{2,1,0:T(8,128)S(1)} %broadcast_multiply_fusion.1), kind=kLoop, calls=%fused_computation.37 | loop fusion | flops 1966080 | bytes 2384896 | tf_op jit(solution)/shard_map/convert_element_type | solution.py:170
  30.7 0.6 convolution_add_fusion
  31.3 0.2 copy-done.65
  31.5 6.8 %fusion.1 = f32[3072,128]{1,0:T(8,128)S(1)} fusion(bf16[256,128]{1,0:T(8,128)(2,1)S(1)} %copy-done.65, f32[3072,256]{1,0:T(8,128)S(1)} %convolution_add_fusion, f32[128]{0:T(128)S(1)} %copy-done.66, f32[128]{0:T(128)S(1)} %copy-done.67), kind=kOutput, calls=%fused_computation.6 | convolution fusion | flops 253231104 | bytes 4785152 | tf_op jit(solution)/shard_map/dot_general | solution.py:177
  38.4 1.4 %convolution_add_fusion.2 = f32[3072,4]{0,1:T(4,128)S(1)} fusion(f32[3072,4]{0,1:T(4,128)S(1)} %fusion.126, f32[3072,128]{1,0:T(8,128)S(1)} %fusion.1, f32[128,4]{0,1:T(4,128)S(1)} %copy-done.10), kind=kOutput, calls=%fused_computation.9 | convolution fusion | flops 18886656 | bytes 1673216 | tf_op jit(solution)/shard_map/dot_general | solution.py:178
  39.8 0.1 reshape.236
  40.0 8.0 %all-gather = f32[6,4,32,32]{3,2,1,0:T(8,128)S(1)} all-gather(f32[3,4,32,32]{3,2,1,0:T(8,128)S(1)} %bitcast.206), channel_id=2, replica_groups=mesh['groups'=2,'tiles'=8,'ens'=2,'lev'=1] {'ens'}, dimensions={0}, use_global_device_ids=true | all-gather | bytes 147456 | tf_op jit(solution)/shard_map/all_gather | solution.py:112
  47.9 0.3 sqrt_reduce_fusion
  48.3 0.3 sqrt_reduce_fusion.1
  48.6 0.7 subtract_reduce_fusion
  49.3 0.1 reshape.237
  49.5 0.9 %fusion.127 = f32[3072,128]{1,0:T(8,128)S(1)} fusion(bf16[3072,4]{0,1:T(4,128)(2,1)S(1)} %reshape.237, f32[128,4]{0,1:T(4,128)S(1)} %copy-done.10), kind=kOutput, calls=%fused_computation.271 | convolution fusion | flops 18874368 | bytes 1599488 | tf_op jit(solution)/shard_map/dot_general | solution.py:126
  50.4 4.7 %multiply_reduce_fusion.1 = (f32[3072]{0:T(1024)S(1)}, f32[3072,128]{1,0:T(8,128)}) fusion(f32[128]{0:T(128)S(1)} %copy-done.11, bf16[128,256]{1,0:T(8,128)(2,1)S(1)} %copy-done, bf16[256,128]{1,0:T(8,128)(2,1)} %param.24, f32[3072,256]{1,0:T(8,128)} %copy-done.2, f32[3072,128]{1,0:T(8,128)S(1)} %fusion.127, f32[128]{0:T(128)S(1)} %copy-done.67), kind=kOutput, calls=%fused_computation.35 | convolution fusion | flops 412873728 | bytes 6435840 | tf_op jit(solution)/shard_map/dot_general | solution.py:185
  55.2 2.7 %multiply_reduce_fusion = f32[3,32,32]{2,1,0:T(8,128)S(1)} fusion(f32[3,32,32,128]{3,2,1,0:T(8,128)} %bitcast.201, f32[3,32,32,128]{3,2,1,0:T(8,128)S(1)} %get-tuple-element.19, f32[128]{0:T(128)S(1)} %copy-done.11, f32[3,32,32]{2,1,0:T(8,128)S(1)} %add_rsqrt_fusion, f32[3,32,32]{2,1,0:T(8,128)S(1)} %broadcast_multiply_fusion.1), kind=kLoop, calls=%fused_computation.34 | loop fusion | flops 1963008 | bytes 3183104 | tf_op jit(solution)/shard_map/reduce_sum | solution.py:198
  57.9 2.0 %multiply_convert_fusion.1 = bf16[3,32,32,128]{3,2,1,0:T(8,128)(2,1)S(1)} fusion(f32[3,32,32,128]{3,2,1,0:T(8,128)S(1)} %bitcast.202, f32[3,32,32,128]{3,2,1,0:T(8,128)S(1)} %get-tuple-element.19, f32[3,32,32]{2,1,0:T(8,128)S(1)} %broadcast_multiply_fusion, f32[3,32,32]{2,1,0:T(8,128)S(1)} %div.51, f32[128]{0:T(128)S(1)} %copy-done.11, ...), kind=kLoop, calls=%fused_computation.33 | loop fusion | flops 3145728 | bytes 3981824 | tf_op jit(solution)/shard_map/convert_element_type | solution.py:200
  60.1 0.2 fusion.33
  60.3 0.2 fusion.31
  60.6 3.5 %collective-permute-start.3 = (bf16[3,32,3,128]{3,2,1,0:T(4,128)(2,1)S(1)}, bf16[3,32,3,128]{3,2,1,0:T(4,128)(2,1)S(1)}, u32[]{:S(2)}, u32[]{:S(2)}) collective-permute-start(bf16[3,32,3,128]{3,2,1,0:T(4,128)(2,1)S(1)} %get-tuple-element.27), channel_id=1, source_target_pairs={{2,0},{4,2},{6,4},{8,6},{10,8},{12,10},{14,12},{0,14},{3,1},{5,3},... | collective-permute-start | bytes 221192 | tf_op jit(solution)/shard_map/ppermute | solution.py:20
  64.1 0.6 fusion.47
  64.7 1.8 %collective-permute-done.2 = bf16[3,32,3,128]{3,2,1,0:T(4,128)(2,1)S(1)} collective-permute-done((bf16[3,32,3,128]{3,2,1,0:T(4,128)(2,1)S(1)}, bf16[3,32,3,128]{3,2,1,0:T(4,128)(2,1)S(1)}, u32[]{:S(2)}, u32[]{:S(2)}) %collective-permute-start.2) | collective-permute-done | bytes 73760 | tf_op jit(solution)/shard_map/ppermute | solution.py:17
  66.5 0.1 fusion.54
  66.7 0.2 fusion.35
  66.9 0.1 fusion.52
  67.1 0.2 fusion.29
  67.4 0.1 fusion.50
  67.5 0.1 fusion.48
  67.8 1.9 %maximum_maximum_fusion.2 = (bf16[3,38,35,128]{3,2,1,0:T(8,128)(2,1)S(1)}, bf16[3,38,35,128]{3,2,1,0:T(8,128)(2,1)S(1)}) fusion(bf16[3,3,32,128]{3,2,1,0:T(8,128)(2,1)S(1)} %copy.148, bf16[3,32,32,128]{3,2,1,0:T(8,128)(2,1)S(1)} %multiply_convert_fusion.1, bf16[3,3,32,128]{3,2,1,0:T(8,128)(2,1)S(1)} %copy.149, bf16[3,3,3,128]{3,2,1,0:T(4,128)(2,1)S(1)} %copy.154, ...), kind=kLoop, calls=%fused_computation.43 | loop fusion | flops 12257280 | bytes 3151872 | tf_op jit(solution)/shard_map/concatenate | solution.py:90
  69.9 15.5 %fusion.28 = bf16[1,1,1,3,32,32,128]{6,5,4,3,2,1,0:T(8,128)(2,1)} fusion(f32[3,32,32,128]{3,2,1,0:T(8,128)S(1)} %bitcast.200, bf16[3,38,35,128]{3,2,1,0:T(8,128)(2,1)S(1)} %get-tuple-element.23, f32[128]{0:T(128)S(1)} %get-tuple-element.42, f32[128]{0:T(128)S(1)} %get-tuple-element.61, f32[128]{0:T(128)S(1)} %copy-done.25, ...), kind=kLoop, calls=%fused_computation.77 | loop fusion | flops 60948480 | bytes 36360704 | tf_op jit(solution)/shard_map/broadcast_in_dim | solution.py:207
  (181 shorter events, 1.3 us)
Async XLA Ops:
  0.6 30.0 %copy-start = (bf16[128,256]{1,0:T(8,128)(2,1)S(1)}, bf16[128,256]{1,0:T(8,128)(2,1)}, u32[]{:S(2)}) copy-start(bf16[128,256]{1,0:T(8,128)(2,1)} %param.22) | copy-start | bytes 196612
  0.6 8.4 %copy-start.8 = (s32[8,3]{0,1:T(4,128)S(1)}, s32[8,3]{0,1:T(4,128)}, u32[]{:S(2)}) copy-start(s32[8,3]{0,1:T(4,128)} %param.15) | copy-start | bytes 292
  0.7 8.6 %copy-start.6 = (s32[1,1,3,32,32]{4,3,2,1,0:T(8,128)S(1)}, s32[1,1,3,32,32]{4,3,2,1,0:T(8,128)}, u32[]{:S(2)}) copy-start(s32[1,1,3,32,32]{4,3,2,1,0:T(8,128)} %param.16) | copy-start | bytes 36868
  0.7 8.6 %copy-start.9 = (f32[7,7,128]{2,1,0:T(8,128)S(1)}, f32[7,7,128]{2,1,0:T(8,128)}, u32[]{:S(2)}) copy-start(f32[7,7,128]{2,1,0:T(8,128)} %param.18) | copy-start | bytes 75268
  0.7 8.9 %copy-start.4 = (bf16[1,1,3,4,32,32]{5,4,3,2,1,0:T(8,128)(2,1)S(1)}, bf16[1,1,3,4,32,32]{5,4,3,2,1,0:T(8,128)(2,1)}, u32[]{:S(2)}) copy-start(bf16[1,1,3,4,32,32]{5,4,3,2,1,0:T(8,128)(2,1)} %param.17) | copy-start | bytes 73732
  0.7 9.0 %copy-start.3 = (bf16[1,1,1,3,32,32,128]{6,5,4,3,2,1,0:T(8,128)(2,1)S(1)}, bf16[1,1,1,3,32,32,128]{6,5,4,3,2,1,0:T(8,128)(2,1)}, u32[]{:S(2)}) copy-start(bf16[1,1,1,3,32,32,128]{6,5,4,3,2,1,0:T(8,128)(2,1)} %param.14) | copy-start | bytes 2359300
  4.4 6.4 %copy-start.10 = (f32[128,4]{0,1:T(4,128)S(1)}, f32[128,4]{0,1:T(4,128)}, u32[]{:S(2)}) copy-start(f32[128,4]{0,1:T(4,128)} %param.27) | copy-start | bytes 6148
  4.4 7.3 %collective-permute-start = (bf16[3,32,3,128]{3,2,1,0:T(4,128)(2,1)S(1)}, bf16[3,32,3,128]{3,2,1,0:T(4,128)(2,1)S(1)}, u32[]{:S(2)}, u32[]{:S(2)}) collective-permute-start(bf16[3,32,3,128]{3,2,1,0:T(4,128)(2,1)S(1)} %get-tuple-element.30), channel_id=1, source_target_pairs={{0,2},{2,4},{4,6},{6,8},{8,10},{10,12},{12,14},{14,0},{1,3},{3,5},... | collective-permute-start | bytes 221192 | tf_op jit(solution)/shard_map/ppermute | solution.py:17
  4.9 7.3 %collective-permute-start.1 = (bf16[3,32,3,128]{3,2,1,0:T(4,128)(2,1)S(1)}, bf16[3,32,3,128]{3,2,1,0:T(4,128)(2,1)S(1)}, u32[]{:S(2)}, u32[]{:S(2)}) collective-permute-start(bf16[3,32,3,128]{3,2,1,0:T(4,128)(2,1)S(1)} %get-tuple-element.31), channel_id=1, source_target_pairs={{2,0},{4,2},{6,4},{8,6},{10,8},{12,10},{14,12},{0,14},{3,1},{5,3},... | collective-permute-start | bytes 221192 | tf_op jit(solution)/shard_map/ppermute | solution.py:20
  9.3 5.4 %copy-start.12 = (f32[128]{0:T(128)}, f32[128]{0:T(128)S(1)}, u32[]{:S(2)}) copy-start(f32[128]{0:T(128)S(1)} %get-tuple-element.74) | copy-start | bytes 1540
  9.3 5.4 %copy-start.14 = (f32[128]{0:T(128)}, f32[128]{0:T(128)S(1)}, u32[]{:S(2)}) copy-start(f32[128]{0:T(128)S(1)} %get-tuple-element.75) | copy-start | bytes 1540
  9.3 5.4 %copy-start.16 = (f32[128]{0:T(128)}, f32[128]{0:T(128)S(1)}, u32[]{:S(2)}) copy-start(f32[128]{0:T(128)S(1)} %get-tuple-element.76) | copy-start | bytes 1540
  9.3 5.4 %copy-start.18 = (f32[128]{0:T(128)}, f32[128]{0:T(128)S(1)}, u32[]{:S(2)}) copy-start(f32[128]{0:T(128)S(1)} %get-tuple-element.77) | copy-start | bytes 1540
  9.3 5.4 %copy-start.20 = (f32[128]{0:T(128)}, f32[128]{0:T(128)S(1)}, u32[]{:S(2)}) copy-start(f32[128]{0:T(128)S(1)} %get-tuple-element.78) | copy-start | bytes 1540
  9.3 5.4 %copy-start.22 = (f32[128]{0:T(128)}, f32[128]{0:T(128)S(1)}, u32[]{:S(2)}) copy-start(f32[128]{0:T(128)S(1)} %get-tuple-element.79) | copy-start | bytes 1540
  10.3 4.4 %copy-start.48 = (pred[3,3]{1,0:T(4,128)(4,1)}, pred[3,3]{1,0:T(4,128)(4,1)S(1)}, u32[]{:S(2)}) copy-start(pred[3,3]{1,0:T(4,128)(4,1)S(1)} %get-tuple-element.103) | copy-start | bytes 31
  10.3 4.4 %copy-start.50 = (pred[3,3]{1,0:T(4,128)(4,1)}, pred[3,3]{1,0:T(4,128)(4,1)S(1)}, u32[]{:S(2)}) copy-start(pred[3,3]{1,0:T(4,128)(4,1)S(1)} %get-tuple-element.96) | copy-start | bytes 31
  10.3 4.4 %copy-start.52 = (pred[3,3]{1,0:T(4,128)(4,1)}, pred[3,3]{1,0:T(4,128)(4,1)S(1)}, u32[]{:S(2)}) copy-start(pred[3,3]{1,0:T(4,128)(4,1)S(1)} %get-tuple-element.97) | copy-start | bytes 31
  10.3 4.4 %copy-start.54 = (pred[3,3]{1,0:T(4,128)(4,1)}, pred[3,3]{1,0:T(4,128)(4,1)S(1)}, u32[]{:S(2)}) copy-start(pred[3,3]{1,0:T(4,128)(4,1)S(1)} %get-tuple-element.98) | copy-start | bytes 31
  10.3 4.4 %copy-start.56 = (pred[3,3]{1,0:T(4,128)(4,1)}, pred[3,3]{1,0:T(4,128)(4,1)S(1)}, u32[]{:S(2)}) copy-start(pred[3,3]{1,0:T(4,128)(4,1)S(1)} %get-tuple-element.101) | copy-start | bytes 31
  10.3 4.4 %copy-start.58 = (pred[3,3]{1,0:T(4,128)(4,1)}, pred[3,3]{1,0:T(4,128)(4,1)S(1)}, u32[]{:S(2)}) copy-start(pred[3,3]{1,0:T(4,128)(4,1)S(1)} %get-tuple-element.102) | copy-start | bytes 31
  11.5 3.3 %copy-start.24 = (f32[128]{0:T(128)}, f32[128]{0:T(128)S(1)}, u32[]{:S(2)}) copy-start(f32[128]{0:T(128)S(1)} %get-tuple-element.80) | copy-start | bytes 1540
  11.5 3.3 %copy-start.26 = (f32[128]{0:T(128)}, f32[128]{0:T(128)S(1)}, u32[]{:S(2)}) copy-start(f32[128]{0:T(128)S(1)} %get-tuple-element.81) | copy-start | bytes 1540
  11.5 3.3 %copy-start.28 = (f32[128]{0:T(128)}, f32[128]{0:T(128)S(1)}, u32[]{:S(2)}) copy-start(f32[128]{0:T(128)S(1)} %get-tuple-element.82) | copy-start | bytes 1540
  11.5 3.3 %copy-start.30 = (f32[128]{0:T(128)}, f32[128]{0:T(128)S(1)}, u32[]{:S(2)}) copy-start(f32[128]{0:T(128)S(1)} %get-tuple-element.83) | copy-start | bytes 1540
  11.5 3.3 %copy-start.32 = (f32[128]{0:T(128)}, f32[128]{0:T(128)S(1)}, u32[]{:S(2)}) copy-start(f32[128]{0:T(128)S(1)} %get-tuple-element.84) | copy-start | bytes 1540
  11.5 3.3 %copy-start.34 = (f32[128]{0:T(128)}, f32[128]{0:T(128)S(1)}, u32[]{:S(2)}) copy-start(f32[128]{0:T(128)S(1)} %get-tuple-element.85) | copy-start | bytes 1540
  11.5 3.3 %copy-start.36 = (f32[128]{0:T(128)}, f32[128]{0:T(128)S(1)}, u32[]{:S(2)}) copy-start(f32[128]{0:T(128)S(1)} %get-tuple-element.86) | copy-start | bytes 1540
  11.6 3.3 %copy-start.38 = (f32[128]{0:T(128)}, f32[128]{0:T(128)S(1)}, u32[]{:S(2)}) copy-start(f32[128]{0:T(128)S(1)} %get-tuple-element.87) | copy-start | bytes 1540
  11.6 3.3 %copy-start.40 = (f32[128]{0:T(128)}, f32[128]{0:T(128)S(1)}, u32[]{:S(2)}) copy-start(f32[128]{0:T(128)S(1)} %get-tuple-element.88) | copy-start | bytes 1540
  11.6 3.3 %copy-start.42 = (f32[128]{0:T(128)}, f32[128]{0:T(128)S(1)}, u32[]{:S(2)}) copy-start(f32[128]{0:T(128)S(1)} %get-tuple-element.89) | copy-start | bytes 1540
  11.6 3.3 %copy-start.44 = (f32[128]{0:T(128)}, f32[128]{0:T(128)S(1)}, u32[]{:S(2)}) copy-start(f32[128]{0:T(128)S(1)} %get-tuple-element.90) | copy-start | bytes 1540
  12.7 2.2 %copy-start.64 = (f32[128]{0:T(128)S(1)}, f32[128]{0:T(128)}, u32[]{:S(2)}) copy-start(f32[128]{0:T(128)} %param.19) | copy-start | bytes 1540
  31.5 6.8 %copy-start.2 = (f32[3072,256]{1,0:T(8,128)}, f32[3072,256]{1,0:T(8,128)S(1)}, u32[]{:S(2)}) copy-start(f32[3072,256]{1,0:T(8,128)S(1)} %convolution_add_fusion) | copy-start | bytes 9437188
  39.9 8.6 %copy-start.5 = (bf16[1,1,3,4,32,32]{5,4,3,2,1,0:T(8,128)(2,1)S(1)}, bf16[1,1,3,4,32,32]{5,4,3,2,1,0:T(8,128)(2,1)}, u32[]{:S(2)}) copy-start(bf16[1,1,3,4,32,32]{5,4,3,2,1,0:T(8,128)(2,1)} %param.17) | copy-start | bytes 73732
  55.2 2.7 %copy-start.1 = (f32[3072,128]{1,0:T(8,128)S(1)}, f32[3072,128]{1,0:T(8,128)}, u32[]{:S(2)}) copy-start(f32[3072,128]{1,0:T(8,128)} %get-tuple-element.109) | copy-start | bytes 4718596
  57.9 2.2 %copy-start.63 = (pred[3,3]{1,0:T(4,128)(4,1)S(1)}, pred[3,3]{1,0:T(4,128)(4,1)}, u32[]{:S(2)}) copy-start(pred[3,3]{1,0:T(4,128)(4,1)} %copy-done.62) | copy-start | bytes 31
  57.9 2.4 %copy-start.61 = (pred[3,3]{1,0:T(4,128)(4,1)S(1)}, pred[3,3]{1,0:T(4,128)(4,1)}, u32[]{:S(2)}) copy-start(pred[3,3]{1,0:T(4,128)(4,1)} %copy-done.60) | copy-start | bytes 31
  57.9 6.2 %copy-start.7 = (f32[3,32,32]{2,1,0:T(8,128)S(1)}, f32[3,32,32]{2,1,0:T(8,128)}, u32[]{:S(2)}) copy-start(f32[3,32,32]{2,1,0:T(8,128)} %get-tuple-element.110) | copy-start | bytes 36868
  59.9 6.6 %copy-start.59 = (pred[3,3]{1,0:T(4,128)(4,1)S(1)}, pred[3,3]{1,0:T(4,128)(4,1)}, u32[]{:S(2)}) copy-start(pred[3,3]{1,0:T(4,128)(4,1)} %copy-done.58) | copy-start | bytes 31
  59.9 6.8 %copy-start.57 = (pred[3,3]{1,0:T(4,128)(4,1)S(1)}, pred[3,3]{1,0:T(4,128)(4,1)}, u32[]{:S(2)}) copy-start(pred[3,3]{1,0:T(4,128)(4,1)} %copy-done.56) | copy-start | bytes 31
  59.9 6.9 %copy-start.55 = (pred[3,3]{1,0:T(4,128)(4,1)S(1)}, pred[3,3]{1,0:T(4,128)(4,1)}, u32[]{:S(2)}) copy-start(pred[3,3]{1,0:T(4,128)(4,1)} %copy-done.54) | copy-start | bytes 31
  59.9 7.2 %copy-start.53 = (pred[3,3]{1,0:T(4,128)(4,1)S(1)}, pred[3,3]{1,0:T(4,128)(4,1)}, u32[]{:S(2)}) copy-start(pred[3,3]{1,0:T(4,128)(4,1)} %copy-done.52) | copy-start | bytes 31
  59.9 7.4 %copy-start.51 = (pred[3,3]{1,0:T(4,128)(4,1)S(1)}, pred[3,3]{1,0:T(4,128)(4,1)}, u32[]{:S(2)}) copy-start(pred[3,3]{1,0:T(4,128)(4,1)} %copy-done.50) | copy-start | bytes 31
  60.0 7.6 %copy-start.49 = (pred[3,3]{1,0:T(4,128)(4,1)S(1)}, pred[3,3]{1,0:T(4,128)(4,1)}, u32[]{:S(2)}) copy-start(pred[3,3]{1,0:T(4,128)(4,1)} %copy-done.48) | copy-start | bytes 31
  60.5 6.0 %collective-permute-start.2 = (bf16[3,32,3,128]{3,2,1,0:T(4,128)(2,1)S(1)}, bf16[3,32,3,128]{3,2,1,0:T(4,128)(2,1)S(1)}, u32[]{:S(2)}, u32[]{:S(2)}) collective-permute-start(bf16[3,32,3,128]{3,2,1,0:T(4,128)(2,1)S(1)} %get-tuple-element.26), channel_id=1, source_target_pairs={{0,2},{2,4},{4,6},{6,8},{8,10},{10,12},{12,14},{14,0},{1,3},{3,5},... | collective-permute-start | bytes 221192 | tf_op jit(solution)/shard_map/ppermute | solution.py:17
  60.6 6.5 %collective-permute-start.3 = (bf16[3,32,3,128]{3,2,1,0:T(4,128)(2,1)S(1)}, bf16[3,32,3,128]{3,2,1,0:T(4,128)(2,1)S(1)}, u32[]{:S(2)}, u32[]{:S(2)}) collective-permute-start(bf16[3,32,3,128]{3,2,1,0:T(4,128)(2,1)S(1)} %get-tuple-element.27), channel_id=1, source_target_pairs={{2,0},{4,2},{6,4},{8,6},{10,8},{12,10},{14,12},{0,14},{3,1},{5,3},... | collective-permute-start | bytes 221192 | tf_op jit(solution)/shard_map/ppermute | solution.py:20
  67.6 2.1 %copy-start.13 = (f32[128]{0:T(128)S(1)}, f32[128]{0:T(128)}, u32[]{:S(2)}) copy-start(f32[128]{0:T(128)} %copy-done.12) | copy-start | bytes 1540
  (24 other events, 41.0 us)
where the time goes:
time: 85.7 us; the launch traced here: 85.4 us
  other arithmetic  44.9 us (52%)
  matrix products  17.7 us (21%)
  starting transfers between devices  8.22 us (10%)
  blocking collectives  7.97 us (9%)
  local copies, waits for them, and re-layouts  2.76 us (3%)
  between operations  2.09 us (2%)
  waiting for transfers between devices  1.8 us (2%)
    broadcast_in_dim x2, other arithmetic, on_device(): return (grad_x[None, None, None], score[None, None])  16.1 us
    reduce_sum x1, other arithmetic, on_device(): mean_z = jnp.mean(conv_out, axis=-1, keepdims=True)  13.6 us
    all_gather x1, blocking collectives, ensemble_terms(): every = lax.all_gather(pred[None], 'ens', axis=0, tiled=True)  7.97 us
    ppermute x2, starting transfers between devices, padded_2(): lax.ppermute(lax.slice_in_dim(block, 0, width, axis=dim), axis, backward)  7.62 us
    dot_general x1, matrix products, on_device(): branch = jnp.dot(act, w_out, preferred_element_type=jnp.float32) + b_out  6.84 us
    dot_general x1, matrix products, on_device(): jnp.dot(grad_pre, w_in.T, preferred_element_type=jnp.float32)  4.72 us
    concatenate x2, other arithmetic, convolve(): jnp.concatenate([left, middle, right], axis=2)  3.82 us
    reduce_sum x1, other arithmetic, on_device(): jnp.mean(gated * normed, axis=-1, keepdims=True)  2.67 us
  transfers between devices with their start and end apart: 4, of which 1 were waited for; matrix products, arithmetic and copies ran while one was open for 4% of the time, Pallas kernels for 0%

commit v1 on v0

v1 whole, which is shorter than its diff:
```python
import functools

import jax
import jax.numpy as jnp
from jax import lax
from jax.experimental import pallas as pl
from jax.experimental.pallas import tpu as pltpu
from jax.sharding import PartitionSpec as P

softness = 0.0625
epsilon = 1e-06
MESH = pl.DeviceIdType.MESH
f32 = jnp.float32
bf16 = jnp.bfloat16
LEFT = 8
NT = (((1,), (1,)), ((), ()))
TN = (((0,), (0,)), ((), ()))


def soft_abs(value):
    return jnp.sqrt(value * value + softness)


def soft_sign(value):
    return value * lax.rsqrt(value * value + softness)


def kernel(
    members,
    columns,
    rows_ref,
    x_ref,
    m8_ref,
    t8_ref,
    dw_ref,
    dwb_ref,
    gain_ref,
    lnb_ref,
    win_ref,
    bin_ref,
    wout_ref,
    bout_ref,
    ls_ref,
    wh8_ref,
    out_ref,
    crps_ref,
    pad,
    lhs,
    band,
    acc,
    normed,
    invs,
    grows,
    mcol,
    xm,
    feat,
    pre,
    act,
    slope,
    ex,
    hx,
    eg,
    hg,
    pmine,
    pall,
    sx,
    rx,
    sg,
    rg,
    sp,
    rp,
    *,
    slots,
    tile,
    size,
):
    rim = size // 2
    half = tile // 2
    width = x_ref.shape[-1]
    nrow = half * tile
    hidden = win_ref.shape[1]
    pairs = (tile + 2 * rim) // 2
    depth = (size + 1) // 2
    me = lax.axis_index("tiles")
    mine = lax.axis_index("ens")
    west = lax.rem(me + columns - 1, columns)
    east = lax.rem(me + 1, columns)

    barrier = pltpu.get_barrier_semaphore()
    pl.semaphore_signal(barrier, inc=1, device_id={"tiles": west}, device_id_type=MESH)
    pl.semaphore_signal(barrier, inc=1, device_id={"tiles": east}, device_id_type=MESH)
    for p in range(1, members):
        pl.semaphore_signal(
            barrier, inc=1, device_id={"ens": lax.rem(mine + p, members)}, device_id_type=MESH
        )

    sub8 = lax.broadcasted_iota(jnp.int32, (8, 1), 0)
    zero_strip = jnp.zeros((size // 2, tile, width), bf16)
    for side in range(2):
        hx[side, slots] = zero_strip
        hg[side, slots] = zero_strip

    def mask_slot(s, carry):
        m8 = m8_ref[s]
        for b in range(2):
            pick = jnp.broadcast_to((sub8 == 4 * b).astype(bf16), (8, width))
            col = lax.dot_general(m8, pick, TN, preferred_element_type=f32)
            mcol[s, b] = col
            xv = x_ref[s, :, b].astype(f32).reshape(nrow, width) * col
            xm[s, b] = xv.astype(bf16)
            x3 = xv.reshape(half, tile, width)
            for r in range(half):
                pad[s, rim + 2 * r + b, LEFT : LEFT + tile, :] = x3[r]
        return carry

    def strips(s, dst):
        for c in range(rim):
            dst[0, s, c] = pad[s, rim : rim + tile, LEFT + tile - rim + c, :].astype(bf16)
            dst[1, s, c] = pad[s, rim : rim + tile, LEFT + c, :].astype(bf16)

    lax.fori_loop(0, slots, mask_slot, 0)
    for s in range(slots):
        strips(s, ex)

    pl.semaphore_wait(barrier, 2 + members - 1)

    def edge_copy(src, dst, send, recv, side):
        return pltpu.make_async_remote_copy(
            src_ref=src,
            dst_ref=dst,
            send_sem=send,
            recv_sem=recv,
            device_id={"tiles": east if side == 0 else west},
            device_id_type=MESH,
        )

    x_copies = [
        edge_copy(ex.at[side], hx.at[side, pl.ds(0, slots)], sx.at[side], rx.at[side], side)
        for side in range(2)
    ]
    for copy in x_copies:
        copy.start()

    eye = lax.broadcasted_iota(jnp.int32, (width, width), 0) == lax.broadcasted_iota(
        jnp.int32, (width, width), 1
    )
    zero_block = jnp.zeros((width, width), bf16)

    def build_band(j, carry):
        for o in range(2 * depth):
            for b in range(2):
                i = o - b
                if 0 <= i < size:
                    row = dw_ref[j, pl.ds(i, 1), :]
                    block = jnp.where(eye, jnp.broadcast_to(row, (width, width)), 0.0).astype(bf16)
                else:
                    block = zero_block
                band[j, o * width : (o + 1) * width, b * width : (b + 1) * width] = block
        return carry

    lax.fori_loop(0, size, build_band, 0)

    wh8 = wh8_ref[...]
    scaled_head = wh8 * ls_ref[...]
    through_head = lax.dot_general(
        scaled_head, wout_ref[...].astype(f32), NT, precision=lax.Precision.HIGHEST,
        preferred_element_type=f32,
    )
    bias_head = jnp.sum(scaled_head * bout_ref[...], axis=1, keepdims=True)
    both = jnp.concatenate([wh8, through_head], axis=1)
    both_hi = both.astype(bf16)
    both_lo = (both - both_hi.astype(f32)).astype(bf16)
    both_hl = jnp.concatenate([both_hi.astype(f32), both_lo.astype(f32)], axis=0).astype(bf16)
    sub16 = lax.broadcasted_iota(jnp.int32, (16, 1), 0)

    own = [rows_ref[me, s] for s in range(slots)]
    wrow = [rows_ref[west, s] for s in range(slots)]
    erow = [rows_ref[east, s] for s in range(slots)]

    def find(source, wanted):
        place = jnp.int32(slots)
        for t in range(slots):
            place = jnp.where((source[t] >= 0) & (source[t] == wanted), jnp.int32(t), place)
        return place

    def vertical():
        edge = jnp.zeros((rim, tile, width), f32)
        for s in range(slots):
            if s > 0:
                flag = ((own[s] >= 0) & (own[s - 1] == own[s] - 1)).astype(f32)
                pad[s, 0:rim, LEFT : LEFT + tile, :] = (
                    pad[s - 1, tile : tile + rim, LEFT : LEFT + tile, :] * flag
                )
            else:
                pad[s, 0:rim, LEFT : LEFT + tile, :] = edge
            if s < slots - 1:
                flag = ((own[s + 1] >= 0) & (own[s + 1] == own[s] + 1)).astype(f32)
                pad[s, tile + rim : tile + 2 * rim, LEFT : LEFT + tile, :] = (
                    pad[s + 1, rim : 2 * rim, LEFT : LEFT + tile, :] * flag
                )
            else:
                pad[s, tile + rim : tile + 2 * rim, LEFT : LEFT + tile, :] = edge

    def lateral(buf):
        for s in range(slots):
            for side, source in ((0, wrow), (1, erow)):
                up = find(source, own[s] - 1)
                level = find(source, own[s])
                down = find(source, own[s] + 1)
                for c in range(rim):
                    at = LEFT - rim + c if side == 0 else LEFT + tile + c
                    pad[s, rim : rim + tile, at, :] = buf[side, level, c].astype(f32)
                    pad[s, 0:rim, at, :] = buf[side, up, c].astype(f32)[tile - rim :]
                    pad[s, tile + rim : tile + 2 * rim, at, :] = buf[side, down, c].astype(f32)[
                        :rim
                    ]

    def conv(s, flip):
        def gather(m, carry):
            for a in range(2):
                lane = (1 - a if flip else a) * width
                for j in range(size):
                    lhs[j, m, :, lane : lane + width] = pad[
                        s, 2 * m + a, LEFT - rim + j : LEFT - rim + j + tile, :
                    ].astype(bf16)
            return carry

        lax.fori_loop(0, pairs, gather, 0)
        total = None
        for j in range(size):
            parts = [
                lhs[j, (depth - 1 - d if flip else d) : (depth - 1 - d if flip else d) + half]
                .reshape(nrow, 2 * width)
                for d in range(depth)
            ]
            part = jnp.dot(
                jnp.concatenate(parts, axis=1),
                band[size - 1 - j if flip else j],
                preferred_element_type=f32,
            )
            if j == 0:
                acc[...] = part
            else:
                acc[...] += part

    vertical()
    for copy in x_copies:
        copy.wait()
    lateral(hx)

    chunk = 64
    nchunk = nrow // chunk

    def pred_copy(s, p):
        return pltpu.make_async_remote_copy(
            src_ref=pmine.at[s],
            dst_ref=pall.at[p - 1, s],
            send_sem=sp.at[p - 1, s],
            recv_sem=rp.at[p - 1, s],
            device_id={"ens": lax.rem(mine + p, members)},
            device_id_type=MESH,
        )

    def forward(s, carry):
        conv(s, False)
        for b in range(2):

            def norm(q, carry):
                at = pl.ds(pl.multiple_of(q * chunk, chunk), chunk)
                z = acc[at, b * width : (b + 1) * width] + dwb_ref[...]
                mean = jnp.mean(z, axis=1, keepdims=True)
                z = z - mean
                inv = lax.rsqrt(jnp.mean(z * z, axis=1, keepdims=True) + epsilon)
                z = z * inv
                normed[s, b, at, :] = z
                invs[s, b, at, :] = jnp.broadcast_to(inv, (chunk, width))
                feat[b, at, :] = (z * gain_ref[...] + lnb_ref[...]).astype(bf16)
                return carry

            lax.fori_loop(0, nchunk, norm, 0, unroll=2)
        res = []
        for b in range(2):
            pre[...] = jnp.dot(feat[b], win_ref[...], preferred_element_type=f32)

            def gelu(q, carry):
                at = pl.ds(pl.multiple_of(q * chunk, chunk), chunk)
                v = pre[at, :] + bin_ref[...]
                cum = 0.5 * (1.0 + lax.erf(v * 0.7071067811865476))
                act[at, :] = (v * cum).astype(bf16)
                slope[s, b, at, :] = cum + v * jnp.exp(-0.5 * v * v) * 0.3989422804014327
                return carry

            lax.fori_loop(0, nchunk, gelu, 0, unroll=2)
            r16 = lax.dot_general(
                both_hl,
                jnp.concatenate([xm[s, b], act[...]], axis=1),
                NT,
                preferred_element_type=f32,
            )
            res.append(r16[:8] + r16[8:])
        pmine[s] = jnp.where(sub8 < 4, res[0], res[1]) + bias_head
        for p in range(1, members):
            pred_copy(s, p).start()
        return carry

    lax.fori_loop(0, slots, forward, 0)

    def gz_copy(s, side):
        return edge_copy(eg.at[side, s], hg.at[side, s], sg.at[side, s], rg.at[side, s], side)

    def backward(s, carry):
        for p in range(1, members):
            pred_copy(s, p).wait()
        every = [pmine[s]] + [pall[p - 1, s] for p in range(1, members)]
        goal = t8_ref[s].astype(f32)
        mask = m8_ref[s].astype(f32)
        skill = soft_abs(every[0] - goal)
        spread = jnp.zeros_like(skill)
        pull = jnp.zeros_like(skill)
        for p in range(1, members):
            skill = skill + soft_abs(every[p] - goal)
            pull = pull + soft_sign(every[0] - every[p])
            for other in range(p):
                spread = spread + soft_abs(every[p] - every[other])
        diagonal = members * softness**0.5
        score = mask * (
            skill / members - (2.0 * spread + diagonal) / (2 * members * members)
        )
        crps_ref[s] = jnp.concatenate(
            [
                jnp.sum(score[:4], axis=0, keepdims=True),
                jnp.sum(score[4:], axis=0, keepdims=True),
            ],
            axis=0,
        )
        gp = mask * (soft_sign(every[0] - goal) / members - pull / (members * members))
        gp = gp.astype(bf16).astype(f32)
        gp16 = jnp.concatenate([gp, gp], axis=0).astype(bf16)
        for b in range(2):
            rows = (lax.rem(sub16, 8) // 4) == b
            wb = jnp.where(rows, both_hl.astype(f32), 0.0).astype(bf16)
            big = lax.dot_general(gp16, wb, TN, preferred_element_type=f32)
            grows[s, b] = big[:, :width]
            pre[...] = big[:, width:]

            def slopes(q, carry):
                at = pl.ds(pl.multiple_of(q * chunk, chunk), chunk)
                act[at, :] = (pre[at, :] * slope[s, b, at, :]).astype(bf16)
                return carry

            lax.fori_loop(0, nchunk, slopes, 0, unroll=2)
            acc[:, b * width : (b + 1) * width] = lax.dot_general(
                act[...], win_ref[...], NT, preferred_element_type=f32
            )
            for r in range(half):
                at = slice(r * tile, (r + 1) * tile)
                g = acc[at, b * width : (b + 1) * width] * gain_ref[...]
                z = normed[s, b, at, :]
                g = invs[s, b, at, :] * (
                    g
                    - jnp.mean(g, axis=1, keepdims=True)
                    - z * jnp.mean(g * z, axis=1, keepdims=True)
                )
                pad[s, rim + 2 * r + b, LEFT : LEFT + tile, :] = g
        strips(s, eg)
        for side in range(2):
            gz_copy(s, side).start()
        return carry

    lax.fori_loop(0, slots, backward, 0)
    vertical()
    for s in range(slots):
        for side in range(2):
            gz_copy(s, side).wait()
    lateral(hg)

    def last(s, carry):
        conv(s, True)
        for b in range(2):
            v = acc[:, (1 - b) * width : (2 - b) * width]
            v = mcol[s, b] * (grows[s, b] + v)
            out_ref[s, :, b] = v.reshape(half, tile, width).astype(bf16)
        return carry

    lax.fori_loop(0, slots, last, 0)


def on_device(
    inputs,
    slot_rows,
    cell_mask,
    target,
    dw_kernel,
    dw_bias,
    ln_gain,
    ln_bias,
    w_in,
    b_in,
    w_out,
    b_out,
    layer_scale,
    w_head,
):
    columns = lax.axis_size("tiles")
    members = lax.axis_size("ens")
    column = lax.axis_index("tiles")
    member = lax.axis_index("ens")
    slots, tile, _, width = inputs.shape[3:]
    size = dw_kernel.shape[0]
    rim = size // 2
    half = tile // 2
    nrow = half * tile
    hidden = w_in.shape[1]
    nv = w_head.shape[1]
    own_rows = lax.dynamic_index_in_dim(slot_rows, column, 0, keepdims=False)
    mask = (cell_mask[0, 0] * (own_rows >= 0)[:, None, None].astype(jnp.int32)).astype(bf16)
    m8 = mask.reshape(slots, half, 2, tile).transpose(0, 2, 1, 3).reshape(slots, 2, 1, nrow)
    m8 = jnp.broadcast_to(m8, (slots, 2, nv, nrow)).reshape(slots, 2 * nv, nrow)
    t8 = target[0, 0].reshape(slots, nv, half, 2, tile).transpose(0, 3, 1, 2, 4)
    t8 = t8.reshape(slots, 2 * nv, nrow)
    wh8 = jnp.concatenate([w_head.T, w_head.T], axis=0)
    vmem = pl.BlockSpec(memory_space=pltpu.VMEM)
    smem = pl.BlockSpec(memory_space=pltpu.SMEM)
    pairs = (tile + 2 * rim) // 2
    depth = (size + 1) // 2
    strip = (2, slots, rim, tile, width)
    halo = (2, slots + 1, rim, tile, width)
    dma = pltpu.SemaphoreType.DMA
    grad, score = pl.pallas_call(
        functools.partial(kernel, members, columns, slots=slots, tile=tile, size=size),
        out_shape=(
            jax.ShapeDtypeStruct((slots, half, 2, tile, width), bf16),
            jax.ShapeDtypeStruct((slots, 2, nrow), f32),
        ),
        in_specs=[smem] + [vmem] * 13,
        out_specs=(vmem, vmem),
        scratch_shapes=[
            pltpu.VMEM((slots, tile + 2 * rim, tile + 16, width), f32),
            pltpu.VMEM((size, pairs, tile, 2 * width), bf16),
            pltpu.VMEM((size, 2 * depth * width, 2 * width), bf16),
            pltpu.VMEM((nrow, 2 * width), f32),
            pltpu.VMEM((slots, 2, nrow, width), f32),
            pltpu.VMEM((slots, 2, nrow, width), f32),
            pltpu.VMEM((slots, 2, nrow, width), f32),
            pltpu.VMEM((slots, 2, nrow, width), f32),
            pltpu.VMEM((slots, 2, nrow, width), bf16),
            pltpu.VMEM((2, nrow, width), bf16),
            pltpu.VMEM((nrow, hidden), f32),
            pltpu.VMEM((nrow, hidden), bf16),
            pltpu.VMEM((slots, 2, nrow, hidden), f32),
            pltpu.VMEM(strip, bf16),
            pltpu.VMEM(halo, bf16),
            pltpu.VMEM(strip, bf16),
            pltpu.VMEM(halo, bf16),
            pltpu.VMEM((slots, 2 * nv, nrow), f32),
            pltpu.VMEM((members - 1, slots, 2 * nv, nrow), f32),
            dma((2,)),
            dma((2,)),
            dma((2, slots)),
            dma((2, slots)),
            dma((members - 1, slots)),
            dma((members - 1, slots)),
        ],
        compiler_params=pltpu.CompilerParams(
            collective_id=0, has_side_effects=True, vmem_limit_bytes=60 * 2**20
        ),
    )(
        slot_rows,
        inputs.reshape(slots, half, 2, tile, width),
        m8,
        t8,
        dw_kernel.transpose(1, 0, 2),
        dw_bias[None],
        ln_gain[None],
        ln_bias[None],
        w_in,
        b_in[None],
        w_out,
        b_out[None],
        layer_scale[None],
        wh8,
    )
    share = half // members
    score = score.reshape(slots, 2, half, tile)
    score = lax.dynamic_slice_in_dim(score, member * share, share, 2)
    score = score.transpose(0, 2, 1, 3).reshape(slots, 2 * share, tile).astype(bf16)
    return (grad.reshape(inputs.shape), score[None, None])


def solution(mesh):
    placed = (
        P("ens", "lev", ("groups", "tiles"), None, None, None, None),
        P("groups", None),
        P("lev", ("groups", "tiles"), None, None, None),
        P("lev", ("groups", "tiles"), None, None, None, None),
    ) + (P(),) * 10
    return jax.shard_map(
        on_device,
        mesh=mesh,
        in_specs=placed,
        out_specs=(
            P("ens", "lev", ("groups", "tiles"), None, None, None, None),
            P("lev", ("groups", "tiles"), None, "ens", None),
        ),
        check_vma=False,
    )
```

time: 85.7 us -> 52.7 us (0.61)
  other arithmetic: 44.9 us -> 1.65 us
  Pallas kernels: 0 us -> 43 us
  matrix products: 17.7 us -> 0 us
  starting transfers between devices: 8.22 us -> 0 us
  blocking collectives: 7.97 us -> 0 us
  local copies, waits for them, and re-layouts: 2.76 us -> 6.94 us
  waiting for transfers between devices: 1.8 us -> 0 us
  between operations: 2.09 us -> 0.7 us
    pallas_call x0 -> x1, Pallas kernels: none -> 43 us  [on_device(): pl.pallas_call(functools.partial(kernel, members, columns, slots=slots, t...]
    reduce_sum x6 -> x0, other arithmetic: 18.5 us -> none  [the longest x1 13.6 us: on_device(): mean_z = jnp.mean(conv_out, axis=-1, keepdims=True)]
    dot_general x22 -> x0, matrix products: 17.7 us -> none  [the longest x1 6.84 us: on_device(): branch = jnp.dot(act, w_out, preferred_element_type=jnp.float32) + b_out]
    broadcast_in_dim x2 -> x0, other arithmetic: 16.1 us -> none  [on_device(): return (grad_x[None, None, None], score[None, None])]
    ppermute x4 -> x0, starting transfers between devices: 8.22 us -> none  [the longest x2 7.62 us: padded_2(): lax.ppermute(lax.slice_in_dim(block, 0, width, axis=dim), axis, backward)]
    all_gather x1 -> x0, blocking collectives: 7.97 us -> none  [ensemble_terms(): every = lax.all_gather(pred[None], 'ens', axis=0, tiled=True)]
    convert_element_type x6 -> x1, other arithmetic: 4.03 us -> 0.18 us  [on_device(): (own_rows >= 0)[:, None, None].astype(jnp.int32)]
    unnamed x136 -> x11, local copies, waits for them, and re-layouts: 0.6 us -> 4.03 us
  transfers between devices with their start and end apart: 4 -> 0, of which waited for: 1 -> 0; matrix products, arithmetic and copies ran while one was open for 4% -> 0% of each run, Pallas kernels for 0% -> 0%
where the time goes in v1:
time: 52.7 us; the launch traced here: 52.3 us
  Pallas kernels  43 us (82%)
  local copies, waits for them, and re-layouts  6.94 us (13%)
  other arithmetic  1.65 us (3%)
  between operations  0.7 us (1%)
    pallas_call x1, Pallas kernels, on_device(): pl.pallas_call(functools.partial(kernel, members, columns, slots=slots, t...  43 us
    unnamed x11, local copies, waits for them, and re-layouts  4.03 us

profile of v1, /device:TPU:0, one launch (start us, length us, event | category | flops | bytes accessed | tf_op | source)
XLA Modules:
  0.0 52.3 jit_solution(17767271417652549948)
XLA Ops:
  0.6 0.0 copy-start.2
  0.6 0.0 copy-start
  0.7 0.7 %copy-done.2 = s32[8,3]{0,1:T(4,128)S(1)} copy-done((s32[8,3]{0,1:T(4,128)S(1)}, s32[8,3]{0,1:T(4,128)}, u32[]{:S(2)}) %copy-start.2) | copy-done | bytes 120
  1.3 0.2 convert_reduce_fusion
  1.5 0.9 %fusion.1 = bf16[3,2,16,32]{3,2,1,0:T(8,128)(2,1)S(1)} fusion(s32[3,16,2,32]{3,2,1,0:T(2,128)} %bitcast.31, s32[3]{0:T(128)S(1)} %convert_reduce_fusion), kind=kLoop, calls=%fused_computation.4 | loop fusion | flops 6144 | bytes 18444 | tf_op jit(solution)/shard_map/transpose | solution.py:417
  2.4 0.1 broadcast_in_dim.27
  2.5 0.6 %reshape.47.m8_ref = bf16[3,8,512]{2,1,0:T(8,128)(2,1)} reshape(bf16[3,2,4,512]{3,2,1,0:T(4,128)(2,1)S(1)} %broadcast_in_dim.28) | data formatting | bytes 49152 | tf_op jit(solution)/shard_map/reshape | solution.py:418
  3.1 0.0 copy-done
  3.1 0.0 copy-start.1
  3.2 0.7 %reshape.48.t8_ref = bf16[3,8,512]{2,1,0:T(8,128)(2,1)} reshape(bf16[3,2,4,16,32]{4,3,2,1,0:T(8,128)(2,1)S(1)} %bitcast.28) | data formatting | bytes 49152 | tf_op jit(solution)/shard_map/reshape | solution.py:420
  3.9 0.0 copy-done.1
  3.9 0.6 %copy.33 = f32[7,7,128]{2,0,1:T(8,128)} copy(f32[7,7,128]{2,1,0:T(8,128)S(1)} %copy-done.1) | data formatting | bytes 50176 | tf_op args[4]
  4.5 0.0 copy-start.3
  4.5 0.7 %copy.23.rows_ref = s32[8,3]{1,0:T(8,128)} copy(s32[8,3]{0,1:T(4,128)S(1)} %copy-done.2) | data formatting | bytes 192 | tf_op args[1]
  5.2 0.0 copy-done.3
  5.2 0.6 %pad_maximum_fusion.wh8_ref = f32[8,128]{1,0:T(8,128)} fusion(f32[4,128]{1,0:T(4,128)S(1)} %bitcast.33), kind=kLoop, calls=%fused_computation.7 | loop fusion | flops 1024 | bytes 6144 | tf_op jit(solution)/shard_map/concatenate | solution.py:421
  5.8 43.0 %shard_map.149 = (bf16[3,16,2,32,128]{4,3,2,1,0:T(8,128)(2,1)}, f32[3,2,512]{2,1,0:T(2,128)}) custom-call(s32[8,3]{1,0:T(8,128)} %copy.23.rows_ref, bf16[3,16,2,32,128]{4,3,2,1,0:T(8,128)(2,1)} %bitcast.27, bf16[3,8,512]{2,1,0:T(8,128)(2,1)} %reshape.47.m8_ref, bf16[3,8,512]{2,1,0:T(8,128)(2,1)} %reshape.48.t8_ref, f32[7,7,128]{2,1,0:T(8,128)} %bitcast.29, ...), custom_call_target="tpu_custom_call" | custom-call | tf_op jit(solution)/shard_map/pallas_call | solution.py:429
  48.8 0.8 %reshape.50 = bf16[3,2,16,32]{3,2,1,0:T(8,128)(2,1)S(1)} reshape(f32[3,2,512]{2,1,0:T(2,128)} %get-tuple-element.5) | data formatting | bytes 18432 | tf_op jit(solution)/shard_map/reshape | solution.py:484
  49.6 0.6 %copy.24 = bf16[3,8,2,32]{3,2,1,0:T(2,128)(2,1)} copy(bf16[3,8,2,32]{3,1,2,0:T(8,128)(2,1)S(1)} %fusion.2) | data formatting | bytes 6144 | tf_op jit(solution)/shard_map/convert_element_type | solution.py:486
  50.2 2.1 %copy.35 = bf16[1,1,1,3,32,32,128]{6,5,4,3,2,1,0:T(8,128)(2,1)} copy(bf16[1,1,1,3,32,32,128]{6,5,4,3,2,1,0:T(8,128)(2,1)} %bitcast.26) | data formatting | bytes 1572864
  (3 shorter events, 0.0 us)
Async XLA Ops:
  0.6 0.7 %copy-start.2 = (s32[8,3]{0,1:T(4,128)S(1)}, s32[8,3]{0,1:T(4,128)}, u32[]{:S(2)}) copy-start(s32[8,3]{0,1:T(4,128)} %param.15) | copy-start | bytes 292
  0.6 2.5 %copy-start = (bf16[1,1,3,4,32,32]{5,4,3,2,1,0:T(8,128)(2,1)S(1)}, bf16[1,1,3,4,32,32]{5,4,3,2,1,0:T(8,128)(2,1)}, u32[]{:S(2)}) copy-start(bf16[1,1,3,4,32,32]{5,4,3,2,1,0:T(8,128)(2,1)} %param.17) | copy-start | bytes 73732
  3.1 0.8 %copy-start.1 = (f32[7,7,128]{2,1,0:T(8,128)S(1)}, f32[7,7,128]{2,1,0:T(8,128)}, u32[]{:S(2)}) copy-start(f32[7,7,128]{2,1,0:T(8,128)} %param.18) | copy-start | bytes 75268
  4.5 0.7 %copy-start.3 = (f32[128,4]{0,1:T(4,128)S(1)}, f32[128,4]{0,1:T(4,128)}, u32[]{:S(2)}) copy-start(f32[128,4]{0,1:T(4,128)} %param.27) | copy-start | bytes 6148

commit v2 on v1

--- a/solution.py
+++ b/solution.py
@@ -30,8 +30,7 @@
     columns,
     rows_ref,
     x_ref,
-    m8_ref,
-    t8_ref,
+    prep_ref,
     dw_ref,
     dwb_ref,
     gain_ref,
@@ -100,8 +99,13 @@
         hx[side, slots] = zero_strip
         hg[side, slots] = zero_strip
 
+    def mask_rows(s):
+        return jnp.where(
+            sub8 < 4, prep_ref[s, 8:9].astype(f32), prep_ref[s, 9:10].astype(f32)
+        )
+
     def mask_slot(s, carry):
-        m8 = m8_ref[s]
+        m8 = mask_rows(s).astype(bf16)
         for b in range(2):
             pick = jnp.broadcast_to((sub8 == 4 * b).astype(bf16), (8, width))
             col = lax.dot_general(m8, pick, TN, preferred_element_type=f32)
@@ -151,11 +155,11 @@
             for b in range(2):
                 i = o - b
                 if 0 <= i < size:
-                    row = dw_ref[j, pl.ds(i, 1), :]
+                    row = dw_ref[i, pl.ds(j, 1), :]
                     block = jnp.where(eye, jnp.broadcast_to(row, (width, width)), 0.0).astype(bf16)
                 else:
                     block = zero_block
-                band[j, o * width : (o + 1) * width, b * width : (b + 1) * width] = block
+                band[j, b, o * width : (o + 1) * width, :] = block
         return carry
 
     lax.fori_loop(0, size, build_band, 0)
@@ -215,35 +219,39 @@
                         :rim
                     ]
 
+    def product(s, j, flip):
+        for a in range(2):
+            for m in range(pairs):
+                lhs[j, a, m] = pad[
+                    s, 2 * m + a, LEFT - rim + j : LEFT - rim + j + tile, :
+                ].astype(bf16)
+        parts = []
+        for d in range(depth):
+            for a in range(2):
+                at = depth - 1 - d if flip else d
+                part = lhs[j, 1 - a if flip else a, at : at + half]
+                parts.append(part.reshape(nrow, width))
+        k = size - 1 - j if flip else j
+        return jnp.dot(
+            jnp.concatenate(parts, axis=1),
+            jnp.concatenate([band[k, 0], band[k, 1]], axis=1),
+            preferred_element_type=f32,
+        )
+
+    def centre(flip):
+        def one(s, carry):
+            acc[s] = product(s, rim, flip)
+            return carry
+
+        lax.fori_loop(0, slots, one, 0)
+
     def conv(s, flip):
-        def gather(m, carry):
-            for a in range(2):
-                lane = (1 - a if flip else a) * width
-                for j in range(size):
-                    lhs[j, m, :, lane : lane + width] = pad[
-                        s, 2 * m + a, LEFT - rim + j : LEFT - rim + j + tile, :
-                    ].astype(bf16)
-            return carry
-
-        lax.fori_loop(0, pairs, gather, 0)
-        total = None
         for j in range(size):
-            parts = [
-                lhs[j, (depth - 1 - d if flip else d) : (depth - 1 - d if flip else d) + half]
-                .reshape(nrow, 2 * width)
-                for d in range(depth)
-            ]
-            part = jnp.dot(
-                jnp.concatenate(parts, axis=1),
-                band[size - 1 - j if flip else j],
-                preferred_element_type=f32,
-            )
-            if j == 0:
-                acc[...] = part
-            else:
-                acc[...] += part
+            if j != rim:
+                acc[s] += product(s, j, flip)
 
     vertical()
+    centre(False)
     for copy in x_copies:
         copy.wait()
     lateral(hx)
@@ -267,7 +275,7 @@
 
             def norm(q, carry):
                 at = pl.ds(pl.multiple_of(q * chunk, chunk), chunk)
-                z = acc[at, b * width : (b + 1) * width] + dwb_ref[...]
+                z = acc[s, at, b * width : (b + 1) * width] + dwb_ref[...]
                 mean = jnp.mean(z, axis=1, keepdims=True)
                 z = z - mean
                 inv = lax.rsqrt(jnp.mean(z * z, axis=1, keepdims=True) + epsilon)
@@ -312,8 +320,8 @@
         for p in range(1, members):
             pred_copy(s, p).wait()
         every = [pmine[s]] + [pall[p - 1, s] for p in range(1, members)]
-        goal = t8_ref[s].astype(f32)
-        mask = m8_ref[s].astype(f32)
+        goal = prep_ref[s, 0:8].astype(f32)
+        mask = mask_rows(s)
         skill = soft_abs(every[0] - goal)
         spread = jnp.zeros_like(skill)
         pull = jnp.zeros_like(skill)
@@ -326,13 +334,15 @@
         score = mask * (
             skill / members - (2.0 * spread + diagonal) / (2 * members * members)
         )
-        crps_ref[s] = jnp.concatenate(
-            [
-                jnp.sum(score[:4], axis=0, keepdims=True),
-                jnp.sum(score[4:], axis=0, keepdims=True),
-            ],
-            axis=0,
-        )
+        share = half // members
+        for b in range(2):
+            total = jnp.sum(score[4 * b : 4 * b + 4], axis=0, keepdims=True)
+            for r in range(share):
+                piece = total[:, r * tile : (r + 1) * tile]
+                for p in range(1, members):
+                    at = (p * share + r) * tile
+                    piece = jnp.where(mine == p, total[:, at : at + tile], piece)
+                crps_ref[s, 2 * r + b : 2 * r + b + 1, :] = piece
         gp = mask * (soft_sign(every[0] - goal) / members - pull / (members * members))
         gp = gp.astype(bf16).astype(f32)
         gp16 = jnp.concatenate([gp, gp], axis=0).astype(bf16)
@@ -349,12 +359,12 @@
                 return carry
 
             lax.fori_loop(0, nchunk, slopes, 0, unroll=2)
-            acc[:, b * width : (b + 1) * width] = lax.dot_general(
+            acc[s, :, b * width : (b + 1) * width] = lax.dot_general(
                 act[...], win_ref[...], NT, preferred_element_type=f32
             )
             for r in range(half):
                 at = slice(r * tile, (r + 1) * tile)
-                g = acc[at, b * width : (b + 1) * width] * gain_ref[...]
+                g = acc[s, at, b * width : (b + 1) * width] * gain_ref[...]
                 z = normed[s, b, at, :]
                 g = invs[s, b, at, :] * (
                     g
@@ -369,6 +379,7 @@
 
     lax.fori_loop(0, slots, backward, 0)
     vertical()
+    centre(True)
     for s in range(slots):
         for side in range(2):
             gz_copy(s, side).wait()
@@ -377,7 +388,7 @@
     def last(s, carry):
         conv(s, True)
         for b in range(2):
-            v = acc[:, (1 - b) * width : (2 - b) * width]
+            v = acc[s, :, (1 - b) * width : (2 - b) * width]
             v = mcol[s, b] * (grows[s, b] + v)
             out_ref[s, :, b] = v.reshape(half, tile, width).astype(bf16)
         return carry
@@ -404,7 +415,6 @@
     columns = lax.axis_size("tiles")
     members = lax.axis_size("ens")
     column = lax.axis_index("tiles")
-    member = lax.axis_index("ens")
     slots, tile, _, width = inputs.shape[3:]
     size = dw_kernel.shape[0]
     rim = size // 2
@@ -414,10 +424,10 @@
     nv = w_head.shape[1]
     own_rows = lax.dynamic_index_in_dim(slot_rows, column, 0, keepdims=False)
     mask = (cell_mask[0, 0] * (own_rows >= 0)[:, None, None].astype(jnp.int32)).astype(bf16)
-    m8 = mask.reshape(slots, half, 2, tile).transpose(0, 2, 1, 3).reshape(slots, 2, 1, nrow)
-    m8 = jnp.broadcast_to(m8, (slots, 2, nv, nrow)).reshape(slots, 2 * nv, nrow)
+    m2 = mask.reshape(slots, half, 2, tile).transpose(0, 2, 1, 3)
     t8 = target[0, 0].reshape(slots, nv, half, 2, tile).transpose(0, 3, 1, 2, 4)
-    t8 = t8.reshape(slots, 2 * nv, nrow)
+    t8 = t8.reshape(slots, 2 * nv, half, tile)
+    prep = jnp.concatenate([t8, m2], axis=1).reshape(slots, 2 * nv + 2, nrow)
     wh8 = jnp.concatenate([w_head.T, w_head.T], axis=0)
     vmem = pl.BlockSpec(memory_space=pltpu.VMEM)
     smem = pl.BlockSpec(memory_space=pltpu.SMEM)
@@ -430,15 +440,15 @@
         functools.partial(kernel, members, columns, slots=slots, tile=tile, size=size),
         out_shape=(
             jax.ShapeDtypeStruct((slots, half, 2, tile, width), bf16),
-            jax.ShapeDtypeStruct((slots, 2, nrow), f32),
+            jax.ShapeDtypeStruct((slots, tile // members, tile), f32),
         ),
-        in_specs=[smem] + [vmem] * 13,
+        in_specs=[smem] + [vmem] * 12,
         out_specs=(vmem, vmem),
         scratch_shapes=[
             pltpu.VMEM((slots, tile + 2 * rim, tile + 16, width), f32),
-            pltpu.VMEM((size, pairs, tile, 2 * width), bf16),
-            pltpu.VMEM((size, 2 * depth * width, 2 * width), bf16),
-            pltpu.VMEM((nrow, 2 * width), f32),
+            pltpu.VMEM((size, 2, pairs, tile, width), bf16),
+            pltpu.VMEM((size, 2, 2 * depth * width, width), bf16),
+            pltpu.VMEM((slots, nrow, 2 * width), f32),
             pltpu.VMEM((slots, 2, nrow, width), f32),
             pltpu.VMEM((slots, 2, nrow, width), f32),
             pltpu.VMEM((slots, 2, nrow, width), f32),
@@ -467,9 +477,8 @@
     )(
         slot_rows,
         inputs.reshape(slots, half, 2, tile, width),
-        m8,
-        t8,
-        dw_kernel.transpose(1, 0, 2),
+        prep,
+        dw_kernel,
         dw_bias[None],
         ln_gain[None],
         ln_bias[None],
@@ -480,11 +489,7 @@
         layer_scale[None],
         wh8,
     )
-    share = half // members
-    score = score.reshape(slots, 2, half, tile)
-    score = lax.dynamic_slice_in_dim(score, member * share, share, 2)
-    score = score.transpose(0, 2, 1, 3).reshape(slots, 2 * share, tile).astype(bf16)
-    return (grad.reshape(inputs.shape), score[None, None])
+    return (grad.reshape(inputs.shape), score.astype(bf16)[None, None])
 
 
 def solution(mesh):

time: 52.7 us -> 49.1 us (0.932)
  Pallas kernels: 43 us -> 39.3 us
  other arithmetic: 1.65 us -> 5.1 us
  local copies, waits for them, and re-layouts: 6.94 us -> 3.66 us
    pallas_call x1, Pallas kernels: 43 us -> 39.3 us  [on_device(): pl.pallas_call(functools.partial(kernel, members, columns, slots=slots, t...]
    reshape x3 -> x0, local copies, waits for them, and re-layouts: 2.17 us -> none  [the longest x1 0.8 us: on_device(): score = score.reshape(slots, 2, half, tile)]
    broadcast_in_dim x0 -> x1, other arithmetic: none -> 1.34 us  [on_device(): return (grad.reshape(inputs.shape), score.astype(bf16)[None, None])]
    concatenate x1, other arithmetic: 0.59 us -> 1.35 us  [on_device(): wh8 = jnp.concatenate([w_head.T, w_head.T], axis=0)]
    convert_element_type x1, other arithmetic: 0.18 us -> 0.9 us  [on_device(): (own_rows >= 0)[:, None, None].astype(jnp.int32)]
    concatenate x0 -> x1, other arithmetic: none -> 0.63 us  [on_device(): prep = jnp.concatenate([t8, m2], axis=1).reshape(slots, 2 * nv + 2, nrow)]
    unnamed x11 -> x4, local copies, waits for them, and re-layouts: 4.03 us -> 3.41 us
    convert_element_type x2 -> x0, local copies, waits for them, and re-layouts: 0.62 us -> none  [on_device(): score.transpose(0, 2, 1, 3).reshape(slots, 2 * share, tile).astype(bf16)]
where the time goes in v2:
time: 49.1 us; the launch traced here: 48.7 us
  Pallas kernels  39.3 us (80%)
  other arithmetic  5.1 us (10%)
  local copies, waits for them, and re-layouts  3.66 us (7%)
  between operations  0.67 us (1%)
    pallas_call x1, Pallas kernels, on_device(): pl.pallas_call(functools.partial(kernel, members, columns, slots=slots, t...  39.3 us
    unnamed x4, local copies, waits for them, and re-layouts  3.41 us
    concatenate x1, other arithmetic, on_device(): wh8 = jnp.concatenate([w_head.T, w_head.T], axis=0)  1.35 us
    broadcast_in_dim x1, other arithmetic, on_device(): return (grad.reshape(inputs.shape), score.astype(bf16)[None, None])  1.34 us

profile of v2, /device:TPU:0, one launch (start us, length us, event | category | flops | bytes accessed | tf_op | source)
XLA Modules:
  0.0 48.7 jit_solution(7379237624750966296)
XLA Ops:
  0.6 0.0 copy-start
  0.6 0.9 %convert_reduce_fusion = s32[3]{0:T(128)S(1)} fusion(s32[8,3]{0,1:T(4,128)} %param.15, s32[]{:T(128)S(6)} %select_n.4), kind=kLoop, calls=%fused_computation.7 | loop fusion | flops 6 | bytes 28 | tf_op jit(solution)/shard_map/convert_element_type | solution.py:426
  1.5 1.4 %pad_maximum_fusion.1.wh8_ref = f32[8,128]{1,0:T(8,128)} fusion(f32[4,128]{1,0:T(4,128)} %bitcast.27), kind=kLoop, calls=%fused_computation.6 | loop fusion | flops 1024 | bytes 6144 | tf_op jit(solution)/shard_map/concatenate | solution.py:431
  2.9 1.3 %copy.18.rows_ref = s32[8,3]{1,0:T(8,128)} copy(s32[8,3]{0,1:T(4,128)} %param.15) | data formatting | bytes 192 | tf_op args[1]
  4.2 0.9 %fusion.1 = bf16[3,2,16,32]{3,2,1,0:T(8,128)(2,1)S(1)} fusion(s32[3,16,2,32]{3,2,1,0:T(2,128)} %bitcast.26, s32[3]{0:T(128)S(1)} %convert_reduce_fusion), kind=kLoop, calls=%fused_computation.4 | loop fusion | flops 6144 | bytes 18444 | tf_op jit(solution)/shard_map/transpose | solution.py:427
  5.1 0.1 concatenate.12
  5.2 0.0 copy-done
  5.3 0.1 concatenate.11
  5.4 0.6 %pad_maximum_fusion.prep_ref = bf16[3,10,512]{2,1,0:T(8,128)(2,1)} fusion(bf16[3,2,512]{2,1,0:T(2,128)(2,1)S(1)} %concatenate.12, bf16[3,8,512]{2,1,0:T(8,128)(2,1)S(1)} %concatenate.11), kind=kLoop, calls=%fused_computation.1 | loop fusion | flops 61440 | bytes 61440 | tf_op jit(solution)/shard_map/concatenate | solution.py:430
  6.0 39.3 %shard_map.149 = (bf16[3,16,2,32,128]{4,3,2,1,0:T(8,128)(2,1)}, f32[3,16,32]{2,1,0:T(8,128)}) custom-call(s32[8,3]{1,0:T(8,128)} %copy.18.rows_ref, bf16[3,16,2,32,128]{4,3,2,1,0:T(8,128)(2,1)} %bitcast.23, bf16[3,10,512]{2,1,0:T(8,128)(2,1)} %pad_maximum_fusion.prep_ref, f32[7,7,128]{2,1,0:T(8,128)} %dw_ref.1, f32[1,128]{1,0:T(1,128)} %bitcast.29, ...), custom_call_target="tpu_custom_call" | custom-call | tf_op jit(solution)/shard_map/pallas_call | solution.py:439
  45.3 1.3 %convert_bitcast_fusion = bf16[1,1,3,16,32]{4,3,2,1,0:T(8,128)(2,1)} fusion(f32[3,16,32]{2,1,0:T(8,128)} %get-tuple-element.5), kind=kLoop, calls=%fused_computation.5 | loop fusion | flops 1536 | bytes 9216 | tf_op jit(solution)/shard_map/broadcast_in_dim | solution.py:492
  46.7 2.1 %copy.27 = bf16[1,1,1,3,32,32,128]{6,5,4,3,2,1,0:T(8,128)(2,1)} copy(bf16[1,1,1,3,32,32,128]{6,5,4,3,2,1,0:T(8,128)(2,1)} %bitcast.22) | data formatting | bytes 1572864
  (1 shorter events, 0.0 us)
Async XLA Ops:
  0.6 4.6 %copy-start = (bf16[1,1,3,4,32,32]{5,4,3,2,1,0:T(8,128)(2,1)S(1)}, bf16[1,1,3,4,32,32]{5,4,3,2,1,0:T(8,128)(2,1)}, u32[]{:S(2)}) copy-start(bf16[1,1,3,4,32,32]{5,4,3,2,1,0:T(8,128)(2,1)} %param.17) | copy-start | bytes 73732
